TPU v7x, 256 devices: a whole 4x4x8 slice. The times are simulated.
256 devices in a mesh: layer: 2 (over core), row: 8 (over z_hi, y), col: 16 (over x, z_lo).
Axes of the slice: x: 4, y: 4, z: 8 (z_hi: 2, z_lo: 4; z = z_hi * 4 + z_lo), core: 2. Of those that a mesh axis runs over, the one named last changes fastest.
Arguments:
- amplitudes: bfloat16 [512, 128, 128], P(('row', 'col')), may hold values from -6 to 6
- integrals: bfloat16 [32768, 128, 128], P(('layer', 'row', 'col')), may hold values from -0.1875 to 0.1875
- amp_index: int32 [4096, 48], P(('layer', 'row', 'col')), may hold values from 0 to 31
- left_index: int32 [4096, 48], P(('layer', 'row', 'col')), may hold values from 0 to 127, as said below
- right_index: int32 [4096, 48], P(('layer', 'row', 'col')), may hold values from 0 to 127, as said below
- dest_col: int32 [2048, 1], P(('row', 'col')), may hold values from 0 to 15; in each aligned block of 16 rows (0 to 15, 16 to 31, ...) at most 2 rows name the same one
- owner_slot: int32 [2048], P(('row', 'col')), may hold values from 0 to 7
Outputs:
- ladder: float32 [1024, 128, 128], P(('row', 'col'))
Inputs may be any that keep to these rules, and one draw needn't show every extreme that they name: `dest_col`: among the 16 result tiles of one index of row and col, no owner column appears more than 2 times, and some column appears exactly 2 times. A term's amplitude tile is number amp_index among the tiles of the devices with the same col index, counted row by row. A term's left and right integral tiles belong to one auxiliary function: left_index // 2 == right_index // 2. right_index // 2 == left_index // 2 for every term.
All inputs are finite; a program needn't handle non-finite values.
Results may differ from a plain program's by a relative error of at most 0.0029.
Values may be sent and summed in bfloat16 or wider, within the bound.
A program may use at most 64 MiB of HBM per device.

v0:
```python
import jax
import jax.numpy as jnp
from jax import lax
from jax.sharding import PartitionSpec as P

OWN = 8
CAP = 2


def select_tiles(stack_flat, picks, count, tile_edge):
    onehot = (picks[:, None] == jnp.arange(count, dtype=jnp.int32)[None, :]).astype(jnp.bfloat16)
    chosen = jnp.dot(onehot, stack_flat, preferred_element_type=jnp.float32).astype(jnp.bfloat16)
    return chosen.reshape(picks.shape[0], tile_edge, tile_edge)


def shards(amplitudes, integrals, amp_index, left_index, right_index, dest_col, owner_slot):
    columns = lax.axis_size("col")
    slot_count = dest_col.shape[0]
    tile_edge = integrals.shape[1]
    gathered = lax.all_gather(amplitudes, "row", axis=0, tiled=True)
    amp_total = gathered.shape[0]
    int_total = integrals.shape[0]
    amp_flat = gathered.reshape(amp_total, tile_edge * tile_edge)
    int_flat = integrals.reshape(int_total, tile_edge * tile_edge)

    def one_slot(operand_list):
        amp_ids, left_ids, right_ids = operand_list
        amp_tiles = select_tiles(amp_flat, amp_ids, amp_total, tile_edge)
        right_tiles = select_tiles(int_flat, right_ids, int_total, tile_edge)
        middle_product = jnp.einsum(
            "tcd,ted->tce", amp_tiles, right_tiles, preferred_element_type=jnp.float32
        ).astype(jnp.bfloat16)
        left_tile_blocks = select_tiles(int_flat, left_ids, int_total, tile_edge)
        return jnp.einsum(
            "dov,dvh->oh", left_tile_blocks, middle_product, preferred_element_type=jnp.float32
        )

    partials = lax.map(one_slot, (amp_index, left_index, right_index))
    target = dest_col[:, 0]
    counter = jnp.arange(slot_count, dtype=jnp.int32)
    earlier = (target[:, None] == target[None, :]) & (counter[None, :] < counter[:, None])
    position_in = jnp.sum(earlier.astype(jnp.int32), axis=1)
    position = target * CAP + position_in
    placing = (position[None, :] == jnp.arange(columns * CAP, dtype=jnp.int32)[:, None]).astype(
        jnp.float32
    )
    buffer = jnp.dot(
        placing,
        partials.reshape(slot_count, tile_edge * tile_edge),
        precision=lax.Precision.HIGHEST,
        preferred_element_type=jnp.float32,
    )
    buffer = buffer.reshape(columns, CAP, tile_edge, tile_edge)
    labels = (
        jnp.full((columns * CAP,), OWN, jnp.int32)
        .at[position]
        .set(owner_slot)
        .reshape(columns, CAP)
    )
    tiles_in, labels_in = (
        lax.all_to_all(buffer, "col", split_axis=0, concat_axis=0, tiled=True),
        lax.all_to_all(labels, "col", split_axis=0, concat_axis=0, tiled=True),
    )
    flattened = tiles_in.reshape(-1, tile_edge * tile_edge)
    owner_mask = (
        labels_in.reshape(-1)[:, None] == jnp.arange(OWN, dtype=jnp.int32)[None, :]
    ).astype(jnp.float32)
    owned_tiles = jnp.dot(
        owner_mask.T, flattened, precision=lax.Precision.HIGHEST, preferred_element_type=jnp.float32
    )
    owned_tiles = lax.psum(owned_tiles, "layer")
    return owned_tiles.reshape(OWN, tile_edge, tile_edge)


def solution(mesh):
    placed = (
        P(("row", "col"), None, None),
        P(("layer", "row", "col"), None, None),
        P(("layer", "row", "col"), None),
        P(("layer", "row", "col"), None),
        P(("layer", "row", "col"), None),
        P(("row", "col"), None),
        P(("row", "col")),
    )
    return jax.shard_map(
        shards, mesh=mesh, in_specs=placed, out_specs=P(("row", "col"), None, None), check_vma=False
    )
```

profile of v0, /device:TPU:1, one launch (start us, length us, event | category | flops | bytes accessed | tf_op | source)
XLA Modules:
  0.0 384.1 jit_solution(10383428219554340299)
XLA Ops:
  10.3 9.0 %all-to-all-start = ((s32[16,1,2]{2,1,0:T(1,128)}), s32[16,1,2]{2,1,0:T(1,128)S(1)}, u32[]{:S(2)}, u32[]{:S(2)}) async-start(s32[16,1,2]{2,1,0:T(1,128)} %bitcast.8), calls=%async_computation | async-start | bytes 16384 | tf_op jit(solution)/shard_map/all_to_all | solution.py:62
  19.3 7.7 %copy.44 = bf16[16,8,128,128]{3,1,2,0:T(8,128)(2,1)} copy(bf16[16,8,128,128]{3,2,1,0:T(8,128)(2,1)} %bitcast.108) | data formatting | bytes 8388608
  27.0 47.3 %all-gather.2.cloned.1.call-done = bf16[32,128,128]{2,1,0:T(8,128)(2,1)} async-done(((bf16[4,128,128]{2,1,0:T(8,128)(2,1)}), bf16[32,128,128]{2,1,0:T(8,128)(2,1)}) %all-gather.2.cloned.1.call-update) | async-done | bytes 1048592 | tf_op jit(solution)/shard_map/all_gather | solution.py:20
  77.2 210.3 %while.10 = (s32[]{:T(128)}, f32[16,128,128]{2,1,0:T(8,128)}, s32[16,48]{1,0:T(8,128)}, bf16[128,16384]{1,0:T(8,128)(2,1)}, s32[16,48]{1,0:T(8,128)}, /*index=5*...) while((s32[]{:T(128)}, f32[16,128,128]{2,1,0:T(8,128)}, s32[16,48]{1,0:T(8,128)}, ...), condition=%wide.region_3.4_spmd, body=%wide.region_2.3_spmd.sunk | while | flops 858797568 | bytes 45156664 | solution.py:38
  86.7 3.7 fusion.58
  91.1 2.9 fusion.54
  99.8 3.7 fusion.58
  113.0 3.7 fusion.58
  117.3 2.9 fusion.54
  126.1 3.7 fusion.58
  130.5 2.9 fusion.54
  139.3 3.7 fusion.58
  152.4 3.7 fusion.58
  156.8 2.9 fusion.54
  165.6 3.7 fusion.58
  169.9 2.9 fusion.54
  178.7 3.7 fusion.58
  183.1 2.9 fusion.54
  191.9 3.7 fusion.58
  205.0 3.7 fusion.58
  209.4 2.9 fusion.54
  218.1 3.7 fusion.58
  222.5 2.9 fusion.54
  231.3 3.7 fusion.58
  235.7 2.9 fusion.54
  244.4 3.7 fusion.58
  257.6 3.7 fusion.58
  270.7 3.7 fusion.58
  283.9 3.7 fusion.58
  292.2 4.5 %all-to-all-start.1 = ((f32[16,2,128,128]{3,2,1,0:T(8,128)}), f32[16,2,128,128]{3,2,1,0:T(8,128)S(1)}, u32[]{:S(2)}, u32[]{:S(2)}) async-start(f32[16,2,128,128]{3,2,1,0:T(8,128)} %copy.18), calls=%async_computation.1 | async-start | bytes 4194304 | tf_op jit(solution)/shard_map/all_to_all | solution.py:61
  298.2 48.2 %all-to-all-done.1 = f32[16,2,128,128]{3,2,1,0:T(8,128)S(1)} async-done(((f32[16,2,128,128]{3,2,1,0:T(8,128)}), f32[16,2,128,128]{3,2,1,0:T(8,128)S(1)}, u32[]{:S(2)}, u32[]{:S(2)}) %all-to-all-start.1) | async-done | bytes 2097184 | tf_op jit(solution)/shard_map/all_to_all | solution.py:61
  349.4 26.0 %all-reduce.2.cloned.1.call-done = f32[8,128,128]{2,1,0:T(8,128)} async-done(((f32[8,128,128]{2,1,0:T(8,128)}), f32[8,128,128]{2,1,0:T(8,128)}) %all-reduce.2.cloned.1.call-update) | async-done | bytes 524304 | tf_op jit(solution)/shard_map/psum | solution.py:71
  (174 shorter events, 142.3 us)
Async XLA Ops:
  6.5 67.8 %all-gather.2.cloned.1.call-start = ((), (), s32[]{:S(2)}) async-start(), calls=%async_computation.2 | async-start | bytes 1179648 | tf_op jit(solution)/shard_map/all_gather | solution.py:20
  10.3 281.9 %all-to-all-start = ((s32[16,1,2]{2,1,0:T(1,128)}), s32[16,1,2]{2,1,0:T(1,128)S(1)}, u32[]{:S(2)}, u32[]{:S(2)}) async-start(s32[16,1,2]{2,1,0:T(1,128)} %bitcast.8), calls=%async_computation | async-start | bytes 16384 | tf_op jit(solution)/shard_map/all_to_all | solution.py:62
  19.3 7.7 %copy-start.1 = (s32[16,1]{0,1:T(1,128)S(1)}, s32[16,1]{0,1:T(1,128)}, u32[]{:S(2)}) copy-start(s32[16,1]{0,1:T(1,128)} %param.14) | copy-start | bytes 196
  81.2 3.1 copy-start
  94.4 3.1 copy-start
  107.5 3.1 copy-start
  120.7 3.1 copy-start
  133.8 3.1 copy-start
  147.0 3.1 copy-start
  160.1 3.1 copy-start
  173.3 3.1 copy-start
  186.4 3.1 copy-start
  199.6 3.1 copy-start
  212.7 3.1 copy-start
  225.8 3.1 copy-start
  239.0 3.1 copy-start
  252.1 3.1 copy-start
  265.3 3.1 copy-start
  278.4 3.1 copy-start
  292.2 54.3 %all-to-all-start.1 = ((f32[16,2,128,128]{3,2,1,0:T(8,128)}), f32[16,2,128,128]{3,2,1,0:T(8,128)S(1)}, u32[]{:S(2)}, u32[]{:S(2)}) async-start(f32[16,2,128,128]{3,2,1,0:T(8,128)} %copy.18), calls=%async_computation.1 | async-start | bytes 4194304 | tf_op jit(solution)/shard_map/all_to_all | solution.py:61
  296.7 78.7 %all-reduce.2.cloned.1.call-start = ((), (), s32[]{:S(2)}) async-start(), calls=%async_computation.3 | async-start | bytes 1048576 | tf_op jit(solution)/shard_map/psum | solution.py:71
Sparse Core Ops, SparseCore 0:
  10.0 64.2 all-gather.1
  349.6 25.8 all-reduce.1
where the time goes:
time: 386 us; the launch traced here: 384 us
  matrix products  153 us (40%)
  waiting for transfers between devices  122 us (32%)
  local copies, waits for them, and re-layouts  78.2 us (20%)
  starting transfers between devices  13.8 us (4%)
  between operations  13.5 us (3%)
    dot_general x48, matrix products, select_tiles(): jnp.dot(onehot, stack_flat, preferred_element_type=jnp.float32)  90.2 us
    dot_general x16, matrix products, one_slot(): jnp.einsum('dov,dvh->oh', left_tile_blocks, middle_product, preferred_ele...  58.6 us
    all_to_all x1, waiting for transfers between devices, shards(): lax.all_to_all(buffer, 'col', split_axis=0, concat_axis=0, tiled=True)  48.2 us
    all_gather x1, waiting for transfers between devices, shards(): gathered = lax.all_gather(amplitudes, 'row', axis=0, tiled=True)  47.3 us
    while x80, local copies, waits for them, and re-layouts  38.3 us
    psum x1, waiting for transfers between devices, shards(): owned_tiles = lax.psum(owned_tiles, 'layer')  26 us
    eq x32, local copies, waits for them, and re-layouts, select_tiles(): picks[:, None] == jnp.arange(count, dtype=jnp.int32)[None, :]  22.5 us
    unnamed x5, local copies, waits for them, and re-layouts  12.5 us
  transfers between devices with their start and end apart: 4, of which 3 were waited for; matrix products, arithmetic and copies ran while one was open for 59% of the time, Pallas kernels for 0%

commit v1 on v0

--- a/solution.py
+++ b/solution.py
@@ -68,7 +68,7 @@
     owned_tiles = jnp.dot(
         owner_mask.T, flattened, precision=lax.Precision.HIGHEST, preferred_element_type=jnp.float32
     )
-    owned_tiles = lax.psum(owned_tiles, "layer")
+    owned_tiles = jnp.sum(lax.all_gather(owned_tiles, "layer"), axis=0)
     return owned_tiles.reshape(OWN, tile_edge, tile_edge)
 
 

time: 386 us -> 372 us (0.964)
  waiting for transfers between devices: 122 us -> 107 us
    psum x1 -> x0, waiting for transfers between devices: 26 us -> none  [shards(): owned_tiles = lax.psum(owned_tiles, 'layer')]
    all_gather x0 -> x1, waiting for transfers between devices: none -> 10.9 us  [shards(): owned_tiles = jnp.sum(lax.all_gather(owned_tiles, 'layer'), axis=0)]
  transfers between devices with their start and end apart: 4 -> 4, of which waited for: 3 -> 3; matrix products, arithmetic and copies ran while one was open for 59% -> 62% of each run, Pallas kernels for 0% -> 0%
where the time goes in v1:
time: 372 us; the launch traced here: 369 us
  matrix products  154 us (41%)
  waiting for transfers between devices  107 us (29%)
  local copies, waits for them, and re-layouts  76.3 us (21%)
  starting transfers between devices  13.8 us (4%)
  between operations  13.5 us (4%)
    dot_general x48, matrix products, select_tiles(): jnp.dot(onehot, stack_flat, preferred_element_type=jnp.float32)  90.2 us
    dot_general x16, matrix products, one_slot(): jnp.einsum('dov,dvh->oh', left_tile_blocks, middle_product, preferred_ele...  58.6 us
    all_to_all x1, waiting for transfers between devices, shards(): lax.all_to_all(buffer, 'col', split_axis=0, concat_axis=0, tiled=True)  48.2 us
    all_gather x1, waiting for transfers between devices, shards(): gathered = lax.all_gather(amplitudes, 'row', axis=0, tiled=True)  47.3 us
    while x80, local copies, waits for them, and re-layouts  38.3 us
    eq x32, local copies, waits for them, and re-layouts, select_tiles(): picks[:, None] == jnp.arange(count, dtype=jnp.int32)[None, :]  22.5 us
    unnamed x5, local copies, waits for them, and re-layouts  11.5 us
    all_gather x1, waiting for transfers between devices, shards(): owned_tiles = jnp.sum(lax.all_gather(owned_tiles, 'layer'), axis=0)  10.9 us
  transfers between devices with their start and end apart: 4, of which 3 were waited for; matrix products, arithmetic and copies ran while one was open for 62% of the time, Pallas kernels for 0%

profile of v1, /device:TPU:1, one launch (start us, length us, event | category | flops | bytes accessed | tf_op | source)
XLA Modules:
  0.0 369.3 jit_solution(8995333401152293739)
XLA Ops:
  10.3 9.0 %all-to-all-start = ((s32[16,1,2]{2,1,0:T(1,128)}), s32[16,1,2]{2,1,0:T(1,128)S(1)}, u32[]{:S(2)}, u32[]{:S(2)}) async-start(s32[16,1,2]{2,1,0:T(1,128)} %bitcast.8), calls=%async_computation | async-start | bytes 16384 | tf_op jit(solution)/shard_map/all_to_all | solution.py:62
  19.3 7.7 %copy.40 = bf16[16,8,128,128]{3,1,2,0:T(8,128)(2,1)} copy(bf16[16,8,128,128]{3,2,1,0:T(8,128)(2,1)} %bitcast.110) | data formatting | bytes 8388608
  27.0 47.3 %all-gather.4.cloned.1.call-done = bf16[32,128,128]{2,1,0:T(8,128)(2,1)} async-done(((bf16[4,128,128]{2,1,0:T(8,128)(2,1)}), bf16[32,128,128]{2,1,0:T(8,128)(2,1)}) %all-gather.4.cloned.1.call-update) | async-done | bytes 1048592 | tf_op jit(solution)/shard_map/all_gather | solution.py:20
  77.2 210.3 %while.10 = (s32[]{:T(128)}, f32[16,128,128]{2,1,0:T(8,128)}, s32[16,48]{1,0:T(8,128)}, bf16[128,16384]{1,0:T(8,128)(2,1)}, s32[16,48]{1,0:T(8,128)}, /*index=5*...) while((s32[]{:T(128)}, f32[16,128,128]{2,1,0:T(8,128)}, s32[16,48]{1,0:T(8,128)}, ...), condition=%wide.region_3.4_spmd, body=%wide.region_2.3_spmd.sunk | while | flops 858797568 | bytes 45156664 | solution.py:38
  86.7 3.7 fusion.55
  91.1 2.9 fusion.51
  99.8 3.7 fusion.55
  113.0 3.7 fusion.55
  117.3 2.9 fusion.51
  126.1 3.7 fusion.55
  130.5 2.9 fusion.51
  139.3 3.7 fusion.55
  152.4 3.7 fusion.55
  156.8 2.9 fusion.51
  165.6 3.7 fusion.55
  169.9 2.9 fusion.51
  178.7 3.7 fusion.55
  183.1 2.9 fusion.51
  191.9 3.7 fusion.55
  205.0 3.7 fusion.55
  209.4 2.9 fusion.51
  218.1 3.7 fusion.55
  222.5 2.9 fusion.51
  231.3 3.7 fusion.55
  235.7 2.9 fusion.51
  244.4 3.7 fusion.55
  257.6 3.7 fusion.55
  270.7 3.7 fusion.55
  283.9 3.7 fusion.55
  292.2 4.5 %all-to-all-start.1 = ((f32[16,2,128,128]{3,2,1,0:T(8,128)}), f32[16,2,128,128]{3,2,1,0:T(8,128)S(1)}, u32[]{:S(2)}, u32[]{:S(2)}) async-start(f32[16,2,128,128]{3,2,1,0:T(8,128)} %copy.15), calls=%async_computation.1 | async-start | bytes 4194304 | tf_op jit(solution)/shard_map/all_to_all | solution.py:61
  298.2 48.2 %all-to-all-done.1 = f32[16,2,128,128]{3,2,1,0:T(8,128)S(1)} async-done(((f32[16,2,128,128]{3,2,1,0:T(8,128)}), f32[16,2,128,128]{3,2,1,0:T(8,128)S(1)}, u32[]{:S(2)}, u32[]{:S(2)}) %all-to-all-start.1) | async-done | bytes 2097184 | tf_op jit(solution)/shard_map/all_to_all | solution.py:61
  349.3 10.9 %all-gather.6.cloned.1.call-done = f32[16,16384]{1,0:T(8,128)} async-done(((f32[8,16384]{1,0:T(8,128)}), f32[16,16384]{1,0:T(8,128)}) %all-gather.6.cloned.1.call-update) | async-done | bytes 1048592 | tf_op jit(solution)/shard_map/all_gather | solution.py:71
  (174 shorter events, 142.5 us)
Async XLA Ops:
  6.5 67.8 %all-gather.4.cloned.1.call-start = ((), (), s32[]{:S(2)}) async-start(), calls=%async_computation.2 | async-start | bytes 1179648 | tf_op jit(solution)/shard_map/all_gather | solution.py:20
  10.3 281.9 %all-to-all-start = ((s32[16,1,2]{2,1,0:T(1,128)}), s32[16,1,2]{2,1,0:T(1,128)S(1)}, u32[]{:S(2)}, u32[]{:S(2)}) async-start(s32[16,1,2]{2,1,0:T(1,128)} %bitcast.8), calls=%async_computation | async-start | bytes 16384 | tf_op jit(solution)/shard_map/all_to_all | solution.py:62
  19.3 7.7 %copy-start.1 = (s32[16,1]{0,1:T(1,128)S(1)}, s32[16,1]{0,1:T(1,128)}, u32[]{:S(2)}) copy-start(s32[16,1]{0,1:T(1,128)} %param.14) | copy-start | bytes 196
  81.2 3.1 copy-start
  94.4 3.1 copy-start
  107.5 3.1 copy-start
  120.7 3.1 copy-start
  133.8 3.1 copy-start
  147.0 3.1 copy-start
  160.1 3.1 copy-start
  173.3 3.1 copy-start
  186.4 3.1 copy-start
  199.6 3.1 copy-start
  212.7 3.1 copy-start
  225.8 3.1 copy-start
  239.0 3.1 copy-start
  252.1 3.1 copy-start
  265.3 3.1 copy-start
  278.4 3.1 copy-start
  292.2 54.3 %all-to-all-start.1 = ((f32[16,2,128,128]{3,2,1,0:T(8,128)}), f32[16,2,128,128]{3,2,1,0:T(8,128)S(1)}, u32[]{:S(2)}, u32[]{:S(2)}) async-start(f32[16,2,128,128]{3,2,1,0:T(8,128)} %copy.15), calls=%async_computation.1 | async-start | bytes 4194304 | tf_op jit(solution)/shard_map/all_to_all | solution.py:61
  296.7 63.4 %all-gather.6.cloned.1.call-start = ((), (), s32[]{:S(2)}) async-start(), calls=%async_computation.3 | async-start | bytes 1572864 | tf_op jit(solution)/shard_map/all_gather | solution.py:71
Sparse Core Ops, SparseCore 0:
  10.0 64.2 all-gather.3
  349.4 10.6 all-gather.5
